TPU v7x, 32 devices: a whole 2x2x4 slice. The times are simulated.
32 devices in a mesh: section: 2 (over x), space: 16 (over z, y, core).
Axes of the slice: x: 2, y: 2, z: 4, core: 2. Of those that a mesh axis runs over, the one named last changes fastest.
Arguments:
- input_tiles: bfloat16 [16, 2, 4, 8, 8, 256], P('space'), may hold values from -6 to 6
- saved_tiles: bfloat16 [16, 2, 32, 4, 4, 128], P('space'), may hold values from -6 to 6
- out_grad_tiles: bfloat16 [16, 2, 64, 2, 2, 64], P('space'), may hold values from -1 to 1
- kernel_first: bfloat16 [32, 4, 3, 3, 3], replicated, may hold values from -0.625 to 0.625
- bias_first: float32 [32], replicated, may hold values from -3 to 3
- kernel_second: bfloat16 [64, 32, 3, 3, 3], replicated, may hold values from -0.21875 to 0.21875
- bias_second: float32 [64], replicated, may hold values from -3 to 3
Outputs:
- grad_kernel_first: float32 [32, 4, 3, 3, 3], replicated
- grad_bias_first: float32 [32], replicated
- grad_kernel_second: float32 [64, 32, 3, 3, 3], replicated
- grad_bias_second: float32 [64], replicated
All inputs are finite; a program needn't handle non-finite values.
Results may differ from a plain program's by a relative error of at most 0.0031.
Values may be sent and summed in bfloat16 or wider, within the bound.
No kernel may reach another device: no remote copies, remote signals or barrier semaphores. Data moves between devices by JAX's collectives and lax.ppermute only.
A program may use at most 128 MiB of HBM per device.

v0:
```python
import jax
import jax.numpy as jnp
from jax import lax
from jax.sharding import PartitionSpec as P

GY = 8


def from_behind(value, axis, steps):
    count = lax.axis_size(axis)
    first, last = (max(0, -steps), min(count, count - steps))
    return lax.ppermute(value, axis, [(source, source + steps) for source in range(first, last)])


def correlate(padded, kernel):
    return lax.conv_general_dilated(
        padded,
        kernel,
        (1, 1, 1),
        "VALID",
        dimension_numbers=("NCDHW", "OIDHW", "NCDHW"),
        preferred_element_type=jnp.float32,
    )


def kernel_grad(padded, grads):
    result = lax.conv_general_dilated(
        padded,
        grads,
        (1, 1, 1),
        "VALID",
        dimension_numbers=("CNDHW", "IODHW", "NCDHW"),
        preferred_element_type=jnp.float32,
    )
    return jnp.transpose(result, (1, 0, 2, 3, 4))


def flipped(kernel):
    return jnp.transpose(kernel[:, :, ::-1, ::-1, ::-1], (1, 0, 2, 3, 4))


def spread_up(grad):
    batch, channels, rows_y, rows_z, rows_x = grad.shape
    value = grad.astype(jnp.float32) * 0.125
    value = jnp.broadcast_to(
        value[:, :, :, None, :, None, :, None], (batch, channels, rows_y, 2, rows_z, 2, rows_x, 2)
    )
    return value.reshape(batch, channels, 2 * rows_y, 2 * rows_z, 2 * rows_x)


def slope(pre):
    return jnp.where(pre > 0, 1.0, 0.3)


def bias_column(bias):
    return bias[None, :, None, None, None]


def widen_last(field):
    return jnp.pad(field, ((0, 0), (0, 0), (0, 0), (0, 0), (1, 1)))


def extend(field):
    grid_z = lax.axis_size("space") // GY
    place = lax.axis_index("space") % grid_z
    last_plane = field[:, :, :, -1:]
    first_plane = field[:, :, :, :1]
    last_plane = jnp.where(place < grid_z - 1, last_plane, jnp.zeros_like(last_plane))
    first_plane = jnp.where(place > 0, first_plane, jnp.zeros_like(first_plane))
    low_z = from_behind(last_plane, "space", 1)
    high_z = from_behind(first_plane, "space", -1)
    wide = jnp.concatenate([low_z, field, high_z], axis=3)
    low_y = from_behind(wide[:, :, -1:], "space", grid_z)
    high_y = from_behind(wide[:, :, :1], "space", -grid_z)
    return widen_last(jnp.concatenate([low_y, wide, high_y], axis=2))


def second_delta(second_ext, cotangent, kernel_second, bias_second):
    pre_two = correlate(second_ext, kernel_second) + bias_column(bias_second)
    return (spread_up(cotangent) * slope(pre_two)).astype(jnp.bfloat16)


def first_grads(first_ext, arrived, kernel_first, bias_first):
    pre_one = correlate(first_ext, kernel_first) + bias_column(bias_first)
    delta_one = (spread_up(arrived) * slope(pre_one)).astype(jnp.bfloat16)
    return (
        kernel_grad(first_ext, delta_one),
        jnp.sum(delta_one, axis=(0, 2, 3, 4), dtype=jnp.float32),
    )


def on_device(
    input_tiles, saved_tiles, out_grad_tiles, kernel_first, bias_first, kernel_second, bias_second
):
    first = input_tiles[0]
    second = saved_tiles[0]
    cotangent = out_grad_tiles[0]
    section = lax.axis_index("section")
    batches = first.shape[0]
    flipped_two = flipped(kernel_second)
    share = batches // lax.axis_size("section")
    offset = section * share
    local_first = lax.dynamic_slice_in_dim(first, offset, share, 0)
    local_second = lax.dynamic_slice_in_dim(second, offset, share, 0)
    local_cot = lax.dynamic_slice_in_dim(cotangent, offset, share, 0)
    second_ext = extend(local_second)
    first_ext = extend(local_first)
    delta_two = second_delta(second_ext, local_cot, kernel_second, bias_second)
    delta_ext = extend(delta_two)
    grad_w_two = kernel_grad(second_ext, delta_two)
    grad_b_two = jnp.sum(delta_two, axis=(0, 2, 3, 4), dtype=jnp.float32)
    back = correlate(delta_ext, flipped_two).astype(jnp.bfloat16)
    grad_w_one, grad_b_one = first_grads(first_ext, back, kernel_first, bias_first)
    total = lax.psum((grad_w_one, grad_b_one, grad_w_two, grad_b_two), ("section", "space"))
    return (total[0], total[1], total[2], total[3])


def solution(mesh):
    placed = (
        P("space", None, None, None, None, None),
        P("space", None, None, None, None, None),
        P("space", None, None, None, None, None),
        P(),
        P(),
        P(),
        P(),
    )
    return jax.shard_map(
        on_device, mesh=mesh, in_specs=placed, out_specs=(P(), P(), P(), P()), check_vma=False
    )
```

profile of v0, /device:TPU:0, one launch (start us, length us, event | category | flops | bytes accessed | tf_op | source)
XLA Modules:
  0.0 405.5 jit_solution(2935043332899590350)
XLA Ops:
  8.2 2.4 collective-permute-start
  13.0 5.2 %collective-permute-start.4 = (bf16[1,32,4,1,128]{4,1,3,2,0:T(8,128)(2,1)S(1)}, bf16[1,32,4,1,128]{4,1,3,2,0:T(8,128)(2,1)S(1)}, u32[]{:S(2)}, u32[]{:S(2)}) collective-permute-start(bf16[1,32,4,1,128]{4,1,3,2,0:T(8,128)(2,1)S(1)} %get-tuple-element.19), channel_id=1, source_target_pairs={{0,1},{1,2},{2,3},{3,4},{4,5},{5,6},{6,7},{7,8},{8,9},{9,10},{10,1... | collective-permute-start | bytes 98312 | tf_op jit(solution)/shard_map/ppermute | solution.py:12
  20.3 9.1 %copy.94 = bf16[1,4,8,8,256]{1,0,4,3,2:T(2,128)(2,1)} copy(bf16[1,4,8,8,256]{4,3,2,1,0:T(8,128)(2,1)S(1)} %dynamic-slice_bitcast_fusion) | data formatting | bytes 262144 | tf_op jit(solution)/shard_map/dynamic_slice | solution.py:103
  30.8 7.0 %pad_maximum_fusion.3 = (bf16[1,4,1,10,256]{1,0,4,3,2:T(2,128)(2,1)}, bf16[1,4,1,10,256]{1,0,4,3,2:T(2,128)(2,1)}) fusion(bf16[1,4,8,1,256]{1,0,4,3,2:T(2,128)(2,1)S(1)} %copy.95, bf16[1,4,8,8,256]{1,0,4,3,2:T(2,128)(2,1)} %copy.94, bf16[1,4,8,1,256]{1,0,4,3,2:T(2,128)(2,1)S(1)} %copy.93), kind=kLoop, calls=%fused_computation.43 | loop fusion | flops 40960 | bytes 204800 | tf_op jit(solution)/shard_map/slice | solution.py:73
  37.9 2.5 copy.96
  40.4 5.9 %collective-permute-start.2 = (bf16[1,4,1,10,256]{4,1,3,2,0:T(4,128)(2,1)S(1)}, bf16[1,4,1,10,256]{4,1,3,2,0:T(4,128)(2,1)S(1)}, u32[]{:S(2)}, u32[]{:S(2)}) collective-permute-start(bf16[1,4,1,10,256]{4,1,3,2,0:T(4,128)(2,1)S(1)} %copy.96), channel_id=1, source_target_pairs={{0,2},{1,3},{2,4},{3,5},{4,6},{5,7},{6,8},{7,9},{8,10},{9,11},{10,... | collective-permute-start | bytes 61448 | tf_op jit(solution)/shard_map/ppermute | solution.py:12
  46.3 2.5 copy.97
  50.1 5.9 %collective-permute-start.6 = (bf16[1,32,1,6,128]{4,1,3,2,0:T(8,128)(2,1)S(1)}, bf16[1,32,1,6,128]{4,1,3,2,0:T(8,128)(2,1)S(1)}, u32[]{:S(2)}, u32[]{:S(2)}) collective-permute-start(bf16[1,32,1,6,128]{4,1,3,2,0:T(8,128)(2,1)S(1)} %get-tuple-element.17), channel_id=1, source_target_pairs={{0,2},{1,3},{2,4},{3,5},{4,6},{5,7},{6,8},{7,9},{8,10},{9,11},{10,... | collective-permute-start | bytes 147464 | tf_op jit(solution)/shard_map/ppermute | solution.py:12
  56.0 1.5 collective-permute-start.7
  57.5 2.2 copy.98
  59.7 2.2 copy.99
  61.8 40.1 %pad_maximum_fusion = bf16[1,4,10,10,256]{1,0,4,3,2:T(2,128)(2,1)} fusion(bf16[1,4,1,10,256]{1,0,4,3,2:T(2,128)(2,1)} %copy.99, bf16[1,4,8,1,256]{1,0,4,3,2:T(2,128)(2,1)S(1)} %copy.95, bf16[1,4,8,8,256]{1,0,4,3,2:T(2,128)(2,1)} %copy.94, bf16[1,4,8,1,256]{1,0,4,3,2:T(2,128)(2,1)S(1)} %copy.93, bf16[1,4,1,10,256]{1,0,4,3,2:T(2,128)(2,1)} %copy.98), kind=kLoop, calls=%fused_computation | loop fusion | flops 409600 | bytes 409600 | tf_op jit(solution)/shard_map/concatenate | solution.py:75
  101.9 23.7 %copy.113 = bf16[1,4,10,10,256]{4,1,3,2,0:T(4,128)(2,1)S(1)} copy(bf16[1,4,10,10,256]{1,0,4,3,2:T(2,128)(2,1)} %pad_maximum_fusion) | data formatting | bytes 409600 | tf_op jit(solution)/shard_map/concatenate | solution.py:75
  126.6 4.3 %copy.115 = bf16[4,10,10,1,8,33]{4,0,5,2,1,3:T(4,128)(2,1)} copy(bf16[4,10,10,1,8,33]{5,4,0,2,1,3:T(8,128)(2,1)S(1)} %reshape.57) | data formatting | bytes 422400 | tf_op jit(solution)/shard_map/conv_general_dilated | solution.py:16
  132.1 20.5 %fusion = f32[8,8,8,33,32]{4,2,3,1,0:T(8,128)S(1)} fusion(f32[32]{0:T(128)S(1)} %copy-done.9, pred[8,33]{0,1:T(8,128)(4,1)S(1)} %copy-done.11, bf16[32,4,3,3,3]{0,1,4,3,2:T(4,128)(2,1)S(1)} %copy-done.8, bf16[4,10,10,1,7,2]{4,0,5,2,1,3:T(4,128)(2,1)S(1)} %slice.64, bf16[4,10,10,1,8,33]{4,0,5,2,1,3:T(4,128)(2,1)} %copy.115), kind=kOutput, calls=%fused_computation.2 | convolution fusion | flops 119619840 | bytes 2392392 | tf_op jit(solution)/shard_map/conv_general_dilated | solution.py:16
  152.6 6.0 %copy.121 = f32[8,8,8,33,32]{4,3,2,1,0:T(8,128)} copy(f32[8,8,8,33,32]{4,2,3,1,0:T(8,128)S(1)} %fusion) | data formatting | bytes 4325376 | tf_op jit(solution)/shard_map/jit(_where)/select_n | solution.py:52
  158.6 9.5 %reshape.76 = f32[8,8,1,264,32]{4,3,1,0,2:T(8,128)} reshape(f32[8,8,8,33,32]{4,3,2,1,0:T(8,128)} %copy.121) | data formatting | bytes 4325376 | tf_op jit(solution)/shard_map/jit(_where)/select_n | solution.py:52
  169.0 1.7 reshape.45
  170.8 3.0 copy.103
  174.8 3.5 fusion.53
  180.0 1.4 broadcast_select_fusion.1
  181.6 2.0 collective-permute-start.8
  185.7 4.7 %copy.119 = bf16[1,32,6,6,128]{1,0,4,3,2:T(2,128)(2,1)S(1)} copy(bf16[1,32,6,6,128]{4,1,3,2,0:T(8,128)(2,1)} %pad_maximum_fusion.4) | data formatting | bytes 589824 | tf_op jit(solution)/shard_map/concatenate | solution.py:75
  193.2 7.7 %collective-permute-start.10 = (bf16[1,64,1,6,128]{4,1,3,2,0:T(8,128)(2,1)}, bf16[1,64,1,6,128]{4,1,3,2,0:T(8,128)(2,1)S(1)}, u32[]{:S(2)}, u32[]{:S(2)}) collective-permute-start(bf16[1,64,1,6,128]{4,1,3,2,0:T(8,128)(2,1)} %get-tuple-element.15), channel_id=1, source_target_pairs={{0,2},{1,3},{2,4},{3,5},{4,6},{5,7},{6,8},{7,9},{8,10},{9,11},{10,... | collective-permute-start | bytes 294920 | tf_op jit(solution)/shard_map/ppermute | solution.py:12
  201.0 1.5 collective-permute-start.11
  202.4 14.7 %fusion.58 = f32[64,32,3,3,3]{0,1,4,3,2:T(8,128)} fusion(bf16[1,32,6,6,128]{1,0,4,3,2:T(2,128)(2,1)S(1)} %copy.119, bf16[1,64,4,4,128]{1,3,4,2,0:T(4,128)(2,1)S(1)} %get-tuple-element.8), kind=kOutput, calls=%fused_computation.50 | convolution fusion | flops 225312768 | bytes 778240 | tf_op jit(solution)/shard_map/transpose | solution.py:35
  220.7 4.3 %fusion.50 = f32[4,4,8,17,32]{4,2,3,1,0:T(8,128)S(1)} fusion(bf16[64,32,3,3,3]{0,1,4,3,2:T(8,128)(2,1)S(1)} %copy-done.7, bf16[64,6,6,1,7,2]{0,4,5,2,1,3:T(8,128)(2,1)S(1)} %slice.62, bf16[64,6,6,1,8,17]{0,4,5,2,1,3:T(8,128)(2,1)S(1)} %copy.110, pred[8,17]{0,1:T(8,128)(4,1)S(1)} %copy-done.12), kind=kOutput, calls=%fused_computation.40 | convolution fusion | flops 243027968 | bytes 1080456 | tf_op jit(solution)/shard_map/conv_general_dilated | solution.py:16
  225.6 7.3 %broadcast_in_dim.41 = f32[32,4,2,4,2,128,2]{0,6,5,4,3,2,1:T(2,128)} broadcast(f32[32,4,4,128]{0,3,2,1:T(8,128)S(1)} %copy.112), dimensions={0,1,3,5} | broadcast | bytes 2359296 | tf_op jit(solution)/shard_map/broadcast_in_dim | solution.py:45
  232.9 7.6 %convert_reduce_fusion = (f32[32]{0:T(128)}, bf16[1,32,8,8,256]{1,4,3,2,0:T(8,128)(2,1)S(1)}) fusion(f32[1,32,8,8,256]{1,4,3,2,0:T(8,128)} %bitcast.76, f32[8,8,1,264,32]{4,3,1,0,2:T(8,128)} %reshape.76), kind=kLoop, calls=%fused_computation.6 | loop fusion | flops 2097120 | bytes 5243008 | tf_op jit(solution)/shard_map/reduce_sum | solution.py:88
  240.5 111.0 %fusion.3 = f32[32,4,3,3,3]{0,1,4,3,2:T(4,128)S(1)} fusion(bf16[1,4,10,10,256]{1,0,4,3,2:T(2,128)(2,1)} %pad_maximum_fusion, bf16[1,32,8,8,256]{1,4,3,2,0:T(8,128)(2,1)S(1)} %get-tuple-element.10), kind=kOutput, calls=%fused_computation.7 | convolution fusion | flops 112951296 | bytes 1267200 | tf_op jit(solution)/shard_map/transpose | solution.py:35
  351.5 44.9 %all-reduce = (f32[32,4,3,3,3]{0,1,4,3,2:T(4,128)}, f32[32]{0:T(128)}, f32[64]{0:T(128)}) all-reduce(f32[32,4,3,3,3]{0,1,4,3,2:T(4,128)S(1)} %fusion.3, f32[32]{0:T(128)S(1)} %copy-done.4, f32[64]{0:T(128)S(1)} %copy-done.5), channel_id=1, replica_groups=mesh['section'=2,'space'=16] {'section','space'}, use_global_device_ids=true, to_apply=%region_0.1 | all-reduce | flops 3552 | bytes 28416 | tf_op jit(solution)/shard_map/psum | solution.py:114
  396.4 1.8 copy.132
  (80 shorter events, 22.9 us)
Async XLA Ops:
  7.2 1.0 copy-start
  7.2 389.2 %all-reduce.3.cloned.1.call-start = ((), (), s32[]{:S(2)}) async-start(), calls=%async_computation | async-start | bytes 884736 | tf_op jit(solution)/shard_map/psum | solution.py:114
  8.2 21.3 %collective-permute-start = (bf16[1,4,8,1,256]{4,2,3,1,0:T(8,128)(2,1)S(1)}, bf16[1,4,8,1,256]{4,2,3,1,0:T(8,128)(2,1)S(1)}, u32[]{:S(2)}, u32[]{:S(2)}) collective-permute-start(bf16[1,4,8,1,256]{4,2,3,1,0:T(8,128)(2,1)S(1)} %copy.91), channel_id=1, source_target_pairs={{0,1},{1,2},{2,3},{3,4},{4,5},{5,6},{6,7},{7,8},{8,9},{9,10},{10,1... | collective-permute-start | bytes 49160 | tf_op jit(solution)/shard_map/ppermute | solution.py:12
  10.7 19.5 %collective-permute-start.1 = (bf16[1,4,8,1,256]{4,2,3,1,0:T(8,128)(2,1)S(1)}, bf16[1,4,8,1,256]{4,2,3,1,0:T(8,128)(2,1)S(1)}, u32[]{:S(2)}, u32[]{:S(2)}) collective-permute-start(bf16[1,4,8,1,256]{4,2,3,1,0:T(8,128)(2,1)S(1)} %copy.92), channel_id=1, source_target_pairs={{1,0},{2,1},{3,2},{4,3},{5,4},{6,5},{7,6},{8,7},{9,8},{10,9},{11,1... | collective-permute-start | bytes 49160 | tf_op jit(solution)/shard_map/ppermute | solution.py:12
  13.0 37.1 %collective-permute-start.4 = (bf16[1,32,4,1,128]{4,1,3,2,0:T(8,128)(2,1)S(1)}, bf16[1,32,4,1,128]{4,1,3,2,0:T(8,128)(2,1)S(1)}, u32[]{:S(2)}, u32[]{:S(2)}) collective-permute-start(bf16[1,32,4,1,128]{4,1,3,2,0:T(8,128)(2,1)S(1)} %get-tuple-element.19), channel_id=1, source_target_pairs={{0,1},{1,2},{2,3},{3,4},{4,5},{5,6},{6,7},{7,8},{8,9},{9,10},{10,1... | collective-permute-start | bytes 98312 | tf_op jit(solution)/shard_map/ppermute | solution.py:12
  18.1 32.0 %collective-permute-start.5 = (bf16[1,32,4,1,128]{4,1,3,2,0:T(8,128)(2,1)S(1)}, bf16[1,32,4,1,128]{4,1,3,2,0:T(8,128)(2,1)S(1)}, u32[]{:S(2)}, u32[]{:S(2)}) collective-permute-start(bf16[1,32,4,1,128]{4,1,3,2,0:T(8,128)(2,1)S(1)} %get-tuple-element.20), channel_id=1, source_target_pairs={{1,0},{2,1},{3,2},{4,3},{5,4},{6,5},{7,6},{8,7},{9,8},{10,9},{11,1... | collective-permute-start | bytes 98312 | tf_op jit(solution)/shard_map/ppermute | solution.py:12
  40.4 17.1 %collective-permute-start.2 = (bf16[1,4,1,10,256]{4,1,3,2,0:T(4,128)(2,1)S(1)}, bf16[1,4,1,10,256]{4,1,3,2,0:T(4,128)(2,1)S(1)}, u32[]{:S(2)}, u32[]{:S(2)}) collective-permute-start(bf16[1,4,1,10,256]{4,1,3,2,0:T(4,128)(2,1)S(1)} %copy.96), channel_id=1, source_target_pairs={{0,2},{1,3},{2,4},{3,5},{4,6},{5,7},{6,8},{7,9},{8,10},{9,11},{10,... | collective-permute-start | bytes 61448 | tf_op jit(solution)/shard_map/ppermute | solution.py:12
  48.8 10.9 %collective-permute-start.3 = (bf16[1,4,1,10,256]{4,1,3,2,0:T(4,128)(2,1)S(1)}, bf16[1,4,1,10,256]{4,1,3,2,0:T(4,128)(2,1)S(1)}, u32[]{:S(2)}, u32[]{:S(2)}) collective-permute-start(bf16[1,4,1,10,256]{4,1,3,2,0:T(4,128)(2,1)S(1)} %copy.97), channel_id=1, source_target_pairs={{2,0},{3,1},{4,2},{5,3},{6,4},{7,5},{8,6},{9,7},{10,8},{11,9},{12,... | collective-permute-start | bytes 61448 | tf_op jit(solution)/shard_map/ppermute | solution.py:12
  50.1 118.0 %collective-permute-start.6 = (bf16[1,32,1,6,128]{4,1,3,2,0:T(8,128)(2,1)S(1)}, bf16[1,32,1,6,128]{4,1,3,2,0:T(8,128)(2,1)S(1)}, u32[]{:S(2)}, u32[]{:S(2)}) collective-permute-start(bf16[1,32,1,6,128]{4,1,3,2,0:T(8,128)(2,1)S(1)} %get-tuple-element.17), channel_id=1, source_target_pairs={{0,2},{1,3},{2,4},{3,5},{4,6},{5,7},{6,8},{7,9},{8,10},{9,11},{10,... | collective-permute-start | bytes 147464 | tf_op jit(solution)/shard_map/ppermute | solution.py:12
  56.0 112.2 %collective-permute-start.7 = (bf16[1,32,1,6,128]{4,1,3,2,0:T(8,128)(2,1)S(1)}, bf16[1,32,1,6,128]{4,1,3,2,0:T(8,128)(2,1)S(1)}, u32[]{:S(2)}, u32[]{:S(2)}) collective-permute-start(bf16[1,32,1,6,128]{4,1,3,2,0:T(8,128)(2,1)S(1)} %get-tuple-element.18), channel_id=1, source_target_pairs={{2,0},{3,1},{4,2},{5,3},{6,4},{7,5},{8,6},{9,7},{10,8},{11,9},{12,... | collective-permute-start | bytes 147464 | tf_op jit(solution)/shard_map/ppermute | solution.py:12
  126.6 5.5 %copy-start.8 = (bf16[32,4,3,3,3]{0,1,4,3,2:T(4,128)(2,1)S(1)}, bf16[32,4,3,3,3]{0,1,4,3,2:T(4,128)(2,1)}, u32[]{:S(2)}) copy-start(bf16[32,4,3,3,3]{0,1,4,3,2:T(4,128)(2,1)} %param.10) | copy-start | bytes 20740
  126.6 5.5 %copy-start.9 = (f32[32]{0:T(128)S(1)}, f32[32]{0:T(128)}, u32[]{:S(2)}) copy-start(f32[32]{0:T(128)} %param.11) | copy-start | bytes 388
  126.6 5.5 %copy-start.11 = (pred[8,33]{0,1:T(8,128)(4,1)S(1)}, pred[8,33]{0,1:T(8,128)(4,1)}, u32[]{:S(2)}) copy-start(pred[8,33]{0,1:T(8,128)(4,1)} %constant.64) | copy-start | bytes 796
  168.2 0.6 copy-start.2
  170.8 4.0 copy-start.6
  170.8 4.0 copy-start.10
  170.8 4.0 copy-start.12
  178.9 6.1 %copy-start.3 = (bf16[1,32,1,6,128]{4,1,3,2,0:T(8,128)(2,1)S(1)}, bf16[1,32,1,6,128]{4,1,3,2,0:T(8,128)(2,1)}, u32[]{:S(2)}) copy-start(bf16[1,32,1,6,128]{4,1,3,2,0:T(8,128)(2,1)} %copy-done.2) | copy-start | bytes 147460
  181.6 8.8 %collective-permute-start.8 = (bf16[1,64,4,1,128]{1,3,4,2,0:T(2,128)(2,1)}, bf16[1,64,4,1,128]{1,3,4,2,0:T(2,128)(2,1)}, u32[]{:S(2)}, u32[]{:S(2)}) collective-permute-start(bf16[1,64,4,1,128]{1,3,4,2,0:T(2,128)(2,1)} %get-tuple-element.13), channel_id=1, source_target_pairs={{0,1},{1,2},{2,3},{3,4},{4,5},{5,6},{6,7},{7,8},{8,9},{9,10},{10,1... | collective-permute-start | bytes 196616 | tf_op jit(solution)/shard_map/ppermute | solution.py:12
  183.6 7.8 %collective-permute-start.9 = (bf16[1,64,4,1,128]{1,3,4,2,0:T(2,128)(2,1)}, bf16[1,64,4,1,128]{1,3,4,2,0:T(2,128)(2,1)}, u32[]{:S(2)}, u32[]{:S(2)}) collective-permute-start(bf16[1,64,4,1,128]{1,3,4,2,0:T(2,128)(2,1)} %get-tuple-element.14), channel_id=1, source_target_pairs={{1,0},{2,1},{3,2},{4,3},{5,4},{6,5},{7,6},{8,7},{9,8},{10,9},{11,1... | collective-permute-start | bytes 196616 | tf_op jit(solution)/shard_map/ppermute | solution.py:12
  193.2 24.0 %collective-permute-start.10 = (bf16[1,64,1,6,128]{4,1,3,2,0:T(8,128)(2,1)}, bf16[1,64,1,6,128]{4,1,3,2,0:T(8,128)(2,1)S(1)}, u32[]{:S(2)}, u32[]{:S(2)}) collective-permute-start(bf16[1,64,1,6,128]{4,1,3,2,0:T(8,128)(2,1)} %get-tuple-element.15), channel_id=1, source_target_pairs={{0,2},{1,3},{2,4},{3,5},{4,6},{5,7},{6,8},{7,9},{8,10},{9,11},{10,... | collective-permute-start | bytes 294920 | tf_op jit(solution)/shard_map/ppermute | solution.py:12
  201.0 16.2 %collective-permute-start.11 = (bf16[1,64,1,6,128]{4,1,3,2,0:T(8,128)(2,1)S(1)}, bf16[1,64,1,6,128]{4,1,3,2,0:T(8,128)(2,1)}, u32[]{:S(2)}, u32[]{:S(2)}) collective-permute-start(bf16[1,64,1,6,128]{4,1,3,2,0:T(8,128)(2,1)S(1)} %get-tuple-element.16), channel_id=1, source_target_pairs={{2,0},{3,1},{4,2},{5,3},{6,4},{7,5},{8,6},{9,7},{10,8},{11,9},{12,... | collective-permute-start | bytes 294920 | tf_op jit(solution)/shard_map/ppermute | solution.py:12
  219.8 0.9 copy-start.7
  240.5 111.0 %copy-start.4 = (f32[32]{0:T(128)S(1)}, f32[32]{0:T(128)}, u32[]{:S(2)}) copy-start(f32[32]{0:T(128)} %get-tuple-element.9) | copy-start | bytes 388
  240.5 111.0 %copy-start.5 = (f32[64]{0:T(128)S(1)}, f32[64]{0:T(128)}, u32[]{:S(2)}) copy-start(f32[64]{0:T(128)} %get-tuple-element.7) | copy-start | bytes 772
  240.5 157.7 %copy-start.1 = (bf16[1,2,4,8,8,256]{5,4,3,2,1,0:T(8,128)(2,1)S(1)}, bf16[1,2,4,8,8,256]{5,4,3,2,1,0:T(8,128)(2,1)}, u32[]{:S(2)}) copy-start(bf16[1,2,4,8,8,256]{5,4,3,2,1,0:T(8,128)(2,1)} %param.7) | copy-start | bytes 786436
Sparse Core Ops, SparseCore 0:
  217.3 131.7 all-reduce.2
where the time goes:
time: 411 us; the launch traced here: 406 us
  matrix products  154 us (37%)
  local copies, waits for them, and re-layouts  93.5 us (23%)
  other arithmetic  60.7 us (15%)
  blocking collectives  44.9 us (11%)
  starting transfers between devices  37.2 us (9%)
  between operations  15.1 us (4%)
    transpose x2, matrix products, kernel_grad(): return jnp.transpose(result, (1, 0, 2, 3, 4))  126 us
    psum x1, blocking collectives, on_device(): lax.psum((grad_w_one, grad_b_one, grad_w_two, grad_b_two), ('section', 's...  44.9 us
    concatenate x4, other arithmetic, extend(): return widen_last(jnp.concatenate([low_y, wide, high_y], axis=2))  41.9 us
    ppermute x12, starting transfers between devices, from_behind(): lax.ppermute(value, axis, [(source, source + steps) for source in range(f...  37.2 us
    concatenate x5, local copies, waits for them, and re-layouts, extend(): return widen_last(jnp.concatenate([low_y, wide, high_y], axis=2))  29.2 us
    conv_general_dilated x3, matrix products, correlate(): lax.conv_general_dilated(padded, kernel, (1, 1, 1), 'VALID', dimension_nu...  28.4 us
    select_n x3, local copies, waits for them, and re-layouts, slope(): return jnp.where(pre > 0, 1.0, 0.3)  15.8 us
    conv_general_dilated x9, local copies, waits for them, and re-layouts, correlate(): lax.conv_general_dilated(padded, kernel, (1, 1, 1), 'VALID', dimension_nu...  12.5 us
  transfers between devices with their start and end apart: 13, of which 0 were waited for; matrix products, arithmetic and copies ran while one was open for 71% of the time, Pallas kernels for 0%

commit v1 on v0

--- a/solution.py
+++ b/solution.py
@@ -111,7 +111,7 @@
     grad_b_two = jnp.sum(delta_two, axis=(0, 2, 3, 4), dtype=jnp.float32)
     back = correlate(delta_ext, flipped_two).astype(jnp.bfloat16)
     grad_w_one, grad_b_one = first_grads(first_ext, back, kernel_first, bias_first)
-    total = lax.psum((grad_w_one, grad_b_one, grad_w_two, grad_b_two), ("section", "space"))
+    total = lax.psum(lax.psum((grad_w_one, grad_b_one, grad_w_two, grad_b_two), "space"), "section")
     return (total[0], total[1], total[2], total[3])
 
 

time: 411 us -> 490 us (1.19)
  waiting for transfers between devices: 0.05 us -> 50.5 us
  blocking collectives: 44.9 us -> 69.2 us
  matrix products: 154 us -> 163 us
    psum x1 -> x2, waiting for transfers between devices: 0.01 us -> 50.4 us  [the longest x1 50.4 us: on_device(): lax.psum((grad_w_one, grad_b_one, grad_w_two, grad_b_two), 'space')]
    psum x1 -> x2, blocking collectives: 44.9 us -> 69.2 us  [the longest x1 60 us: on_device(): lax.psum((grad_w_one, grad_b_one, grad_w_two, grad_b_two), 'space')]
    transpose x2, matrix products: 126 us -> 135 us  [kernel_grad(): return jnp.transpose(result, (1, 0, 2, 3, 4))]
  transfers between devices with their start and end apart: 13 -> 14, of which waited for: 0 -> 1; matrix products, arithmetic and copies ran while one was open for 71% -> 61% of each run, Pallas kernels for 0% -> 0%
where the time goes in v1:
time: 490 us; the launch traced here: 485 us
  matrix products  163 us (33%)
  local copies, waits for them, and re-layouts  91.7 us (19%)
  blocking collectives  69.2 us (14%)
  other arithmetic  58.5 us (12%)
  waiting for transfers between devices  50.5 us (10%)
  starting transfers between devices  37.1 us (8%)
  between operations  15.1 us (3%)
    transpose x2, matrix products, kernel_grad(): return jnp.transpose(result, (1, 0, 2, 3, 4))  135 us
    psum x1, blocking collectives, on_device(): lax.psum((grad_w_one, grad_b_one, grad_w_two, grad_b_two), 'space')  60 us
    psum x1, waiting for transfers between devices, on_device(): lax.psum((grad_w_one, grad_b_one, grad_w_two, grad_b_two), 'space')  50.4 us
    concatenate x4, other arithmetic, extend(): return widen_last(jnp.concatenate([low_y, wide, high_y], axis=2))  40.3 us
    ppermute x12, starting transfers between devices, from_behind(): lax.ppermute(value, axis, [(source, source + steps) for source in range(f...  37 us
    conv_general_dilated x3, matrix products, correlate(): lax.conv_general_dilated(padded, kernel, (1, 1, 1), 'VALID', dimension_nu...  28 us
    concatenate x5, local copies, waits for them, and re-layouts, extend(): return widen_last(jnp.concatenate([low_y, wide, high_y], axis=2))  26.5 us
    select_n x3, local copies, waits for them, and re-layouts, slope(): return jnp.where(pre > 0, 1.0, 0.3)  15.8 us
  transfers between devices with their start and end apart: 14, of which 1 were waited for; matrix products, arithmetic and copies ran while one was open for 61% of the time, Pallas kernels for 0%

profile of v1, /device:TPU:0, one launch (start us, length us, event | category | flops | bytes accessed | tf_op | source)
XLA Modules:
  0.0 484.9 jit_solution(7398800802604551089)
XLA Ops:
  8.2 2.4 collective-permute-start
  13.0 5.2 %collective-permute-start.4 = (bf16[1,32,4,1,128]{4,1,3,2,0:T(8,128)(2,1)S(1)}, bf16[1,32,4,1,128]{4,1,3,2,0:T(8,128)(2,1)S(1)}, u32[]{:S(2)}, u32[]{:S(2)}) collective-permute-start(bf16[1,32,4,1,128]{4,1,3,2,0:T(8,128)(2,1)S(1)} %get-tuple-element.22), channel_id=1, source_target_pairs={{0,1},{1,2},{2,3},{3,4},{4,5},{5,6},{6,7},{7,8},{8,9},{9,10},{10,1... | collective-permute-start | bytes 98312 | tf_op jit(solution)/shard_map/ppermute | solution.py:12
  20.3 9.1 %copy.94 = bf16[1,4,8,8,256]{1,0,4,3,2:T(2,128)(2,1)} copy(bf16[1,4,8,8,256]{4,3,2,1,0:T(8,128)(2,1)S(1)} %dynamic-slice_bitcast_fusion) | data formatting | bytes 262144 | tf_op jit(solution)/shard_map/dynamic_slice | solution.py:103
  30.8 7.0 %pad_maximum_fusion.3 = (bf16[1,4,1,10,256]{1,0,4,3,2:T(2,128)(2,1)}, bf16[1,4,1,10,256]{1,0,4,3,2:T(2,128)(2,1)}) fusion(bf16[1,4,8,1,256]{1,0,4,3,2:T(2,128)(2,1)S(1)} %copy.95, bf16[1,4,8,8,256]{1,0,4,3,2:T(2,128)(2,1)} %copy.94, bf16[1,4,8,1,256]{1,0,4,3,2:T(2,128)(2,1)S(1)} %copy.93), kind=kLoop, calls=%fused_computation.43 | loop fusion | flops 40960 | bytes 204800 | tf_op jit(solution)/shard_map/slice | solution.py:73
  37.9 2.5 copy.96
  40.4 5.9 %collective-permute-start.2 = (bf16[1,4,1,10,256]{4,1,3,2,0:T(4,128)(2,1)S(1)}, bf16[1,4,1,10,256]{4,1,3,2,0:T(4,128)(2,1)S(1)}, u32[]{:S(2)}, u32[]{:S(2)}) collective-permute-start(bf16[1,4,1,10,256]{4,1,3,2,0:T(4,128)(2,1)S(1)} %copy.96), channel_id=1, source_target_pairs={{0,2},{1,3},{2,4},{3,5},{4,6},{5,7},{6,8},{7,9},{8,10},{9,11},{10,... | collective-permute-start | bytes 61448 | tf_op jit(solution)/shard_map/ppermute | solution.py:12
  46.3 2.5 copy.97
  50.1 5.9 %collective-permute-start.6 = (bf16[1,32,1,6,128]{4,1,3,2,0:T(8,128)(2,1)S(1)}, bf16[1,32,1,6,128]{4,1,3,2,0:T(8,128)(2,1)S(1)}, u32[]{:S(2)}, u32[]{:S(2)}) collective-permute-start(bf16[1,32,1,6,128]{4,1,3,2,0:T(8,128)(2,1)S(1)} %get-tuple-element.20), channel_id=1, source_target_pairs={{0,2},{1,3},{2,4},{3,5},{4,6},{5,7},{6,8},{7,9},{8,10},{9,11},{10,... | collective-permute-start | bytes 147464 | tf_op jit(solution)/shard_map/ppermute | solution.py:12
  57.5 2.2 copy.98
  59.7 2.2 copy.99
  61.8 40.1 %pad_maximum_fusion = bf16[1,4,10,10,256]{1,0,4,3,2:T(2,128)(2,1)} fusion(bf16[1,4,1,10,256]{1,0,4,3,2:T(2,128)(2,1)} %copy.99, bf16[1,4,8,1,256]{1,0,4,3,2:T(2,128)(2,1)S(1)} %copy.95, bf16[1,4,8,8,256]{1,0,4,3,2:T(2,128)(2,1)} %copy.94, bf16[1,4,8,1,256]{1,0,4,3,2:T(2,128)(2,1)S(1)} %copy.93, bf16[1,4,1,10,256]{1,0,4,3,2:T(2,128)(2,1)} %copy.98), kind=kLoop, calls=%fused_computation | loop fusion | flops 409600 | bytes 409600 | tf_op jit(solution)/shard_map/concatenate | solution.py:75
  101.9 23.7 %copy.113 = bf16[1,4,10,10,256]{4,1,3,2,0:T(4,128)(2,1)S(1)} copy(bf16[1,4,10,10,256]{1,0,4,3,2:T(2,128)(2,1)} %pad_maximum_fusion) | data formatting | bytes 409600 | tf_op jit(solution)/shard_map/concatenate | solution.py:75
  126.6 4.3 copy.115
  130.9 1.8 slice.64
  133.6 1.7 reshape.45
  135.3 3.0 copy.103
  139.3 3.5 fusion.53
  145.9 2.0 collective-permute-start.8
  149.3 2.0 copy.119
  151.2 23.9 %fusion.58 = f32[64,32,3,3,3]{0,1,4,3,2:T(8,128)} fusion(bf16[1,32,6,6,128]{1,0,4,3,2:T(2,128)(2,1)S(1)} %copy.119, bf16[1,64,4,4,128]{1,3,4,2,0:T(4,128)(2,1)S(1)} %get-tuple-element.11), kind=kOutput, calls=%fused_computation.50 | convolution fusion | flops 225312768 | bytes 778240 | tf_op jit(solution)/shard_map/transpose | solution.py:35
  177.7 7.7 %collective-permute-start.10 = (bf16[1,64,1,6,128]{4,1,3,2,0:T(8,128)(2,1)S(1)}, bf16[1,64,1,6,128]{4,1,3,2,0:T(8,128)(2,1)S(1)}, u32[]{:S(2)}, u32[]{:S(2)}) collective-permute-start(bf16[1,64,1,6,128]{4,1,3,2,0:T(8,128)(2,1)S(1)} %get-tuple-element.18), channel_id=1, source_target_pairs={{0,2},{1,3},{2,4},{3,5},{4,6},{5,7},{6,8},{7,9},{8,10},{9,11},{10,... | collective-permute-start | bytes 294920 | tf_op jit(solution)/shard_map/ppermute | solution.py:12
  186.8 20.2 %fusion = f32[8,8,8,33,32]{4,2,3,1,0:T(8,128)S(1)} fusion(f32[32]{0:T(128)S(1)} %copy-done.11, pred[8,33]{0,1:T(8,128)(4,1)S(1)} %copy-done.12, bf16[32,4,3,3,3]{0,1,4,3,2:T(4,128)(2,1)S(1)} %copy-done.9, bf16[4,10,10,1,7,2]{4,0,5,2,1,3:T(4,128)(2,1)S(1)} %copy-done.2, bf16[4,10,10,1,8,33]{4,0,5,2,1,3:T(4,128)(2,1)} %copy.115), kind=kOutput, calls=%fused_computation.2 | convolution fusion | flops 119619840 | bytes 2392392 | tf_op jit(solution)/shard_map/conv_general_dilated | solution.py:16
  207.0 6.0 %copy.121 = f32[8,8,8,33,32]{4,3,2,1,0:T(8,128)} copy(f32[8,8,8,33,32]{4,2,3,1,0:T(8,128)S(1)} %fusion) | data formatting | bytes 4325376 | tf_op jit(solution)/shard_map/jit(_where)/select_n | solution.py:52
  213.0 9.5 %reshape.76 = f32[8,8,1,264,32]{4,3,1,0,2:T(8,128)} reshape(f32[8,8,8,33,32]{4,3,2,1,0:T(8,128)} %copy.121) | data formatting | bytes 4325376 | tf_op jit(solution)/shard_map/jit(_where)/select_n | solution.py:52
  222.5 50.4 %all-reduce.5.cloned.1.call-done = f32[64,32,3,3,3]{0,1,4,3,2:T(8,128)} async-done(((f32[64,32,3,3,3]{0,1,4,3,2:T(8,128)}), f32[64,32,3,3,3]{0,1,4,3,2:T(8,128)}) %all-reduce.5.cloned.1.call-update) | async-done | bytes 221200 | tf_op jit(solution)/shard_map/psum | solution.py:114
  275.9 4.3 fusion.50
  280.7 7.3 %broadcast_in_dim.41 = f32[32,4,2,4,2,128,2]{0,6,5,4,3,2,1:T(2,128)} broadcast(f32[32,4,4,128]{0,3,2,1:T(8,128)S(1)} %copy.112), dimensions={0,1,3,5} | broadcast | bytes 2359296 | tf_op jit(solution)/shard_map/broadcast_in_dim | solution.py:45
  288.0 7.6 %convert_reduce_fusion = (f32[32]{0:T(128)}, bf16[1,32,8,8,256]{1,4,3,2,0:T(8,128)(2,1)S(1)}) fusion(f32[1,32,8,8,256]{1,4,3,2,0:T(8,128)} %bitcast.76, f32[8,8,1,264,32]{4,3,1,0,2:T(8,128)} %reshape.76), kind=kLoop, calls=%fused_computation.6 | loop fusion | flops 2097120 | bytes 5243008 | tf_op jit(solution)/shard_map/reduce_sum | solution.py:88
  295.6 111.0 %fusion.3 = f32[32,4,3,3,3]{0,1,4,3,2:T(4,128)S(1)} fusion(bf16[1,4,10,10,256]{1,0,4,3,2:T(2,128)(2,1)} %pad_maximum_fusion, bf16[1,32,8,8,256]{1,4,3,2,0:T(8,128)(2,1)S(1)} %get-tuple-element.13), kind=kOutput, calls=%fused_computation.7 | convolution fusion | flops 112951296 | bytes 1267200 | tf_op jit(solution)/shard_map/transpose | solution.py:35
  406.6 60.0 %all-reduce = (f32[32,4,3,3,3]{0,1,4,3,2:T(4,128)S(1)}, f32[32]{0:T(128)S(1)}, f32[64]{0:T(128)S(1)}) all-reduce(f32[32,4,3,3,3]{0,1,4,3,2:T(4,128)S(1)} %fusion.3, f32[32]{0:T(128)S(1)} %copy-done.5, f32[64]{0:T(128)S(1)} %copy-done.6), channel_id=1, replica_groups=mesh['section'=2,'space'=16] {'space'}, use_global_device_ids=true, to_apply=%region_0.1 | all-reduce | flops 3552 | bytes 28416 | tf_op jit(solution)/shard_map/psum | solution.py:114
  466.6 9.2 %all-reduce.1 = (f32[32,4,3,3,3]{0,1,4,3,2:T(4,128)}, f32[32]{0:T(128)}, f32[64]{0:T(128)}) all-reduce(f32[32,4,3,3,3]{0,1,4,3,2:T(4,128)S(1)} %get-tuple-element.4, f32[32]{0:T(128)S(1)} %get-tuple-element.5, f32[64]{0:T(128)S(1)} %get-tuple-element.6), channel_id=1, replica_groups=mesh['section'=2,'space'=16] {'section'}, use_global_device_ids=true, to_apply=%region_1.2 | all-reduce | flops 3552 | bytes 28416 | tf_op jit(solution)/shard_map/psum | solution.py:114
  475.8 1.8 copy.133
  (88 shorter events, 24.0 us)
Async XLA Ops:
  7.2 1.0 copy-start
  7.2 265.8 %all-reduce.5.cloned.1.call-start = ((), (), s32[]{:S(2)}) async-start(), calls=%async_computation | async-start | bytes 884736 | tf_op jit(solution)/shard_map/psum | solution.py:114
  8.2 21.3 %collective-permute-start = (bf16[1,4,8,1,256]{4,2,3,1,0:T(8,128)(2,1)S(1)}, bf16[1,4,8,1,256]{4,2,3,1,0:T(8,128)(2,1)S(1)}, u32[]{:S(2)}, u32[]{:S(2)}) collective-permute-start(bf16[1,4,8,1,256]{4,2,3,1,0:T(8,128)(2,1)S(1)} %copy.91), channel_id=1, source_target_pairs={{0,1},{1,2},{2,3},{3,4},{4,5},{5,6},{6,7},{7,8},{8,9},{9,10},{10,1... | collective-permute-start | bytes 49160 | tf_op jit(solution)/shard_map/ppermute | solution.py:12
  10.7 19.5 %collective-permute-start.1 = (bf16[1,4,8,1,256]{4,2,3,1,0:T(8,128)(2,1)S(1)}, bf16[1,4,8,1,256]{4,2,3,1,0:T(8,128)(2,1)S(1)}, u32[]{:S(2)}, u32[]{:S(2)}) collective-permute-start(bf16[1,4,8,1,256]{4,2,3,1,0:T(8,128)(2,1)S(1)} %copy.92), channel_id=1, source_target_pairs={{1,0},{2,1},{3,2},{4,3},{5,4},{6,5},{7,6},{8,7},{9,8},{10,9},{11,1... | collective-permute-start | bytes 49160 | tf_op jit(solution)/shard_map/ppermute | solution.py:12
  13.0 37.1 %collective-permute-start.4 = (bf16[1,32,4,1,128]{4,1,3,2,0:T(8,128)(2,1)S(1)}, bf16[1,32,4,1,128]{4,1,3,2,0:T(8,128)(2,1)S(1)}, u32[]{:S(2)}, u32[]{:S(2)}) collective-permute-start(bf16[1,32,4,1,128]{4,1,3,2,0:T(8,128)(2,1)S(1)} %get-tuple-element.22), channel_id=1, source_target_pairs={{0,1},{1,2},{2,3},{3,4},{4,5},{5,6},{6,7},{7,8},{8,9},{9,10},{10,1... | collective-permute-start | bytes 98312 | tf_op jit(solution)/shard_map/ppermute | solution.py:12
  18.1 32.0 %collective-permute-start.5 = (bf16[1,32,4,1,128]{4,1,3,2,0:T(8,128)(2,1)S(1)}, bf16[1,32,4,1,128]{4,1,3,2,0:T(8,128)(2,1)S(1)}, u32[]{:S(2)}, u32[]{:S(2)}) collective-permute-start(bf16[1,32,4,1,128]{4,1,3,2,0:T(8,128)(2,1)S(1)} %get-tuple-element.23), channel_id=1, source_target_pairs={{1,0},{2,1},{3,2},{4,3},{5,4},{6,5},{7,6},{8,7},{9,8},{10,9},{11,1... | collective-permute-start | bytes 98312 | tf_op jit(solution)/shard_map/ppermute | solution.py:12
  40.4 17.1 %collective-permute-start.2 = (bf16[1,4,1,10,256]{4,1,3,2,0:T(4,128)(2,1)S(1)}, bf16[1,4,1,10,256]{4,1,3,2,0:T(4,128)(2,1)S(1)}, u32[]{:S(2)}, u32[]{:S(2)}) collective-permute-start(bf16[1,4,1,10,256]{4,1,3,2,0:T(4,128)(2,1)S(1)} %copy.96), channel_id=1, source_target_pairs={{0,2},{1,3},{2,4},{3,5},{4,6},{5,7},{6,8},{7,9},{8,10},{9,11},{10,... | collective-permute-start | bytes 61448 | tf_op jit(solution)/shard_map/ppermute | solution.py:12
  48.8 10.9 %collective-permute-start.3 = (bf16[1,4,1,10,256]{4,1,3,2,0:T(4,128)(2,1)S(1)}, bf16[1,4,1,10,256]{4,1,3,2,0:T(4,128)(2,1)S(1)}, u32[]{:S(2)}, u32[]{:S(2)}) collective-permute-start(bf16[1,4,1,10,256]{4,1,3,2,0:T(4,128)(2,1)S(1)} %copy.97), channel_id=1, source_target_pairs={{2,0},{3,1},{4,2},{5,3},{6,4},{7,5},{8,6},{9,7},{10,8},{11,9},{12,... | collective-permute-start | bytes 61448 | tf_op jit(solution)/shard_map/ppermute | solution.py:12
  50.1 82.6 %collective-permute-start.6 = (bf16[1,32,1,6,128]{4,1,3,2,0:T(8,128)(2,1)S(1)}, bf16[1,32,1,6,128]{4,1,3,2,0:T(8,128)(2,1)S(1)}, u32[]{:S(2)}, u32[]{:S(2)}) collective-permute-start(bf16[1,32,1,6,128]{4,1,3,2,0:T(8,128)(2,1)S(1)} %get-tuple-element.20), channel_id=1, source_target_pairs={{0,2},{1,3},{2,4},{3,5},{4,6},{5,7},{6,8},{7,9},{8,10},{9,11},{10,... | collective-permute-start | bytes 147464 | tf_op jit(solution)/shard_map/ppermute | solution.py:12
  56.0 76.7 %collective-permute-start.7 = (bf16[1,32,1,6,128]{4,1,3,2,0:T(8,128)(2,1)S(1)}, bf16[1,32,1,6,128]{4,1,3,2,0:T(8,128)(2,1)S(1)}, u32[]{:S(2)}, u32[]{:S(2)}) collective-permute-start(bf16[1,32,1,6,128]{4,1,3,2,0:T(8,128)(2,1)S(1)} %get-tuple-element.21), channel_id=1, source_target_pairs={{2,0},{3,1},{4,2},{5,3},{6,4},{7,5},{8,6},{9,7},{10,8},{11,9},{12,... | collective-permute-start | bytes 147464 | tf_op jit(solution)/shard_map/ppermute | solution.py:12
  132.7 0.6 copy-start.3
  135.3 4.0 copy-start.7
  135.3 4.0 copy-start.10
  135.3 4.0 copy-start.13
  143.1 6.1 %copy-start.4 = (bf16[1,32,1,6,128]{4,1,3,2,0:T(8,128)(2,1)S(1)}, bf16[1,32,1,6,128]{4,1,3,2,0:T(8,128)(2,1)}, u32[]{:S(2)}) copy-start(bf16[1,32,1,6,128]{4,1,3,2,0:T(8,128)(2,1)} %copy-done.3) | copy-start | bytes 147460
  145.9 29.6 %collective-permute-start.8 = (bf16[1,64,4,1,128]{1,3,4,2,0:T(2,128)(2,1)}, bf16[1,64,4,1,128]{1,3,4,2,0:T(2,128)(2,1)}, u32[]{:S(2)}, u32[]{:S(2)}) collective-permute-start(bf16[1,64,4,1,128]{1,3,4,2,0:T(2,128)(2,1)} %get-tuple-element.16), channel_id=1, source_target_pairs={{0,1},{1,2},{2,3},{3,4},{4,5},{5,6},{6,7},{7,8},{8,9},{9,10},{10,1... | collective-permute-start | bytes 196616 | tf_op jit(solution)/shard_map/ppermute | solution.py:12
  147.9 28.7 %collective-permute-start.9 = (bf16[1,64,4,1,128]{1,3,4,2,0:T(2,128)(2,1)}, bf16[1,64,4,1,128]{1,3,4,2,0:T(2,128)(2,1)}, u32[]{:S(2)}, u32[]{:S(2)}) collective-permute-start(bf16[1,64,4,1,128]{1,3,4,2,0:T(2,128)(2,1)} %get-tuple-element.17), channel_id=1, source_target_pairs={{1,0},{2,1},{3,2},{4,3},{5,4},{6,5},{7,6},{8,7},{9,8},{10,9},{11,1... | collective-permute-start | bytes 196616 | tf_op jit(solution)/shard_map/ppermute | solution.py:12
  175.1 11.6 %copy-start.2 = (bf16[4,10,10,1,7,2]{4,0,5,2,1,3:T(4,128)(2,1)S(1)}, bf16[4,10,10,1,7,2]{4,0,5,2,1,3:T(4,128)(2,1)}, u32[]{:S(2)}) copy-start(bf16[4,10,10,1,7,2]{4,0,5,2,1,3:T(4,128)(2,1)} %slice.64) | copy-start | bytes 33604
  175.2 11.6 %copy-start.9 = (bf16[32,4,3,3,3]{0,1,4,3,2:T(4,128)(2,1)S(1)}, bf16[32,4,3,3,3]{0,1,4,3,2:T(4,128)(2,1)}, u32[]{:S(2)}) copy-start(bf16[32,4,3,3,3]{0,1,4,3,2:T(4,128)(2,1)} %param.10) | copy-start | bytes 20740
  175.2 11.6 %copy-start.11 = (f32[32]{0:T(128)S(1)}, f32[32]{0:T(128)}, u32[]{:S(2)}) copy-start(f32[32]{0:T(128)} %param.11) | copy-start | bytes 388
  175.2 11.6 %copy-start.12 = (pred[8,33]{0,1:T(8,128)(4,1)S(1)}, pred[8,33]{0,1:T(8,128)(4,1)}, u32[]{:S(2)}) copy-start(pred[8,33]{0,1:T(8,128)(4,1)} %constant.64) | copy-start | bytes 796
  175.5 300.4 %all-reduce.7.cloned.1.call-start = ((), (), s32[]{:S(2)}) async-start(), calls=%async_computation.1 | async-start | bytes 884736 | tf_op jit(solution)/shard_map/psum | solution.py:114
  177.7 95.3 %collective-permute-start.10 = (bf16[1,64,1,6,128]{4,1,3,2,0:T(8,128)(2,1)S(1)}, bf16[1,64,1,6,128]{4,1,3,2,0:T(8,128)(2,1)S(1)}, u32[]{:S(2)}, u32[]{:S(2)}) collective-permute-start(bf16[1,64,1,6,128]{4,1,3,2,0:T(8,128)(2,1)S(1)} %get-tuple-element.18), channel_id=1, source_target_pairs={{0,2},{1,3},{2,4},{3,5},{4,6},{5,7},{6,8},{7,9},{8,10},{9,11},{10,... | collective-permute-start | bytes 294920 | tf_op jit(solution)/shard_map/ppermute | solution.py:12
  185.5 87.5 %collective-permute-start.11 = (bf16[1,64,1,6,128]{4,1,3,2,0:T(8,128)(2,1)S(1)}, bf16[1,64,1,6,128]{4,1,3,2,0:T(8,128)(2,1)S(1)}, u32[]{:S(2)}, u32[]{:S(2)}) collective-permute-start(bf16[1,64,1,6,128]{4,1,3,2,0:T(8,128)(2,1)S(1)} %get-tuple-element.19), channel_id=1, source_target_pairs={{2,0},{3,1},{4,2},{5,3},{6,4},{7,5},{8,6},{9,7},{10,8},{11,9},{12,... | collective-permute-start | bytes 294920 | tf_op jit(solution)/shard_map/ppermute | solution.py:12
  274.9 0.9 copy-start.8
  274.9 0.9 copy-start.14
  295.6 111.0 %copy-start.5 = (f32[32]{0:T(128)S(1)}, f32[32]{0:T(128)}, u32[]{:S(2)}) copy-start(f32[32]{0:T(128)} %get-tuple-element.12) | copy-start | bytes 388
  295.6 111.0 %copy-start.6 = (f32[64]{0:T(128)S(1)}, f32[64]{0:T(128)}, u32[]{:S(2)}) copy-start(f32[64]{0:T(128)} %get-tuple-element.10) | copy-start | bytes 772
  295.6 182.0 %copy-start.1 = (bf16[1,2,4,8,8,256]{5,4,3,2,1,0:T(8,128)(2,1)S(1)}, bf16[1,2,4,8,8,256]{5,4,3,2,1,0:T(8,128)(2,1)}, u32[]{:S(2)}) copy-start(bf16[1,2,4,8,8,256]{5,4,3,2,1,0:T(8,128)(2,1)} %param.7) | copy-start | bytes 786436
Sparse Core Ops, SparseCore 0:
  175.6 97.3 all-reduce.4
  275.2 27.2 all-reduce.6
